TPU v7x, 32 devices: a whole 2x2x4 slice. The times are simulated.
32 devices in a mesh: enc: 4 (over x, core), row: 4 (over z), col: 2 (over y).
Axes of the slice: x: 2, y: 2, z: 4, core: 2. Of those that a mesh axis runs over, the one named last changes fastest.
Arguments:
- out_grad: bfloat16 [48, 8192], P(None, ('enc', 'col')), may hold values from -6 to 6
- gate_pre: bfloat16 [48, 29568], P('enc', 'row'), may hold values from -6 to 6
- up_pre: bfloat16 [48, 29568], P('enc', 'row'), may hold values from -6 to 6
- w_gate: bfloat16 [8192, 29568], P(('enc', 'col'), 'row'), may hold values from -0.0625 to 0.0625
- w_up: bfloat16 [8192, 29568], P(('enc', 'col'), 'row'), may hold values from -0.0625 to 0.0625
- w_down: bfloat16 [29568, 8192], P('row', ('enc', 'col')), may hold values from -0.03125 to 0.03125
- w_proj: bfloat16 [12800, 8192], P(None, ('enc', 'col')), may hold values from -0.0546875 to 0.0546875
- enc_hidden: bfloat16 [192, 6400], P('row', ('enc', 'col')), may hold values from -6 to 6
- route: int32 [48], replicated, may hold values from 0 to 47, each once
- img_count: int32 [4], replicated, may hold values from 1 to 12
Outputs:
- enc_grad: bfloat16 [3200, 6400], P(None, ('enc', 'col'))
Inputs may be any that keep to these rules, and one draw needn't show every extreme that they name: route[12 * r + k] is the language row that holds slot k of row group r; every language row appears once. Slots k of row group r with k >= img_count[r] are empty.
All inputs are finite; a program needn't handle non-finite values.
Results may differ from a plain program's by a relative error of at most 0.02.
Values may be sent and summed in bfloat16 or wider, within the bound.
No kernel may reach another device: no remote copies, remote signals or barrier semaphores. Data moves between devices by JAX's collectives and lax.ppermute only.
A program may use at most 128 MiB of HBM per device.

v0:
```python
import math
import jax
import jax.numpy as jnp
from jax import lax
from jax.sharding import PartitionSpec as P

SHUF = 4
IMG = 12


def contract_last(left, right):
    return lax.dot_general(
        left, right, (((1,), (1,)), ((), ())), preferred_element_type=jnp.float32
    )


def contract_first(left, right):
    return lax.dot_general(
        left, right, (((0,), (0,)), ((), ())), preferred_element_type=jnp.float32
    )


def gate_grads(hidden_grad, gate_pre, up_pre):
    share_rows = hidden_grad.shape[0]
    offset = lax.axis_index("col") * share_rows
    gate_vals = lax.dynamic_slice_in_dim(gate_pre, offset, share_rows, 0).astype(jnp.float32)
    up_vals = lax.dynamic_slice_in_dim(up_pre, offset, share_rows, 0).astype(jnp.float32)
    squash = jax.nn.sigmoid(gate_vals)
    grad_gate = (hidden_grad * up_vals * squash * (1.0 + gate_vals * (1.0 - squash))).astype(
        jnp.bfloat16
    )
    grad_up = (hidden_grad * gate_vals * squash).astype(jnp.bfloat16)
    return (grad_gate, grad_up)


def shards(out_grad, gate_pre, up_pre, w_gate, w_up, w_down, w_proj, enc_hidden, route, img_count):
    hidden_part = contract_last(out_grad, w_down)
    enc_share = lax.psum_scatter(hidden_part, "enc", scatter_dimension=0, tiled=True)
    hidden_grad = lax.psum_scatter(enc_share, "col", scatter_dimension=0, tiled=True)
    grad_gate, grad_up = gate_grads(hidden_grad, gate_pre, up_pre)
    grad_gate, grad_up = (
        lax.all_gather(grad_gate, "col", axis=0, tiled=True),
        lax.all_gather(grad_up, "col", axis=0, tiled=True),
    )
    grad_gate, grad_up = (
        lax.all_gather(grad_gate, "enc", axis=0, tiled=True),
        lax.all_gather(grad_up, "enc", axis=0, tiled=True),
    )
    routed_gate = jnp.take(grad_gate, route, axis=0)
    routed_up = jnp.take(grad_up, route, axis=0)
    input_part = contract_last(routed_gate, w_gate) + contract_last(routed_up, w_up)
    positions = jnp.arange(route.shape[0], dtype=jnp.int32)
    alive_mask = positions % IMG < jnp.repeat(img_count, IMG)
    input_part = jnp.where(alive_mask[:, None], input_part, jnp.zeros_like(input_part))
    image_grad = lax.psum_scatter(input_part, "row", scatter_dimension=0, tiled=True).astype(
        jnp.bfloat16
    )
    shuffled_grad = lax.psum_scatter(
        contract_last(image_grad, w_proj), ("enc", "col"), scatter_dimension=1, tiled=True
    )
    feature_share = shuffled_grad.shape[1] // SHUF
    patch_grad = (
        shuffled_grad.reshape(IMG, feature_share, SHUF)
        .transpose(0, 2, 1)
        .reshape(IMG * SHUF, feature_share)
        .astype(jnp.bfloat16)
    )
    patch_total = enc_hidden.shape[0] * lax.axis_size("row")
    scale = 1.0 / math.sqrt(patch_total)
    group_term = (
        contract_first(lax.all_gather(patch_grad, ("enc", "col"), axis=1, tiled=True), enc_hidden)
        * scale
    )
    total = lax.psum(group_term.astype(jnp.bfloat16), "row")
    return total


def solution(mesh):
    placed = (
        P(None, ("enc", "col")),
        P("enc", "row"),
        P("enc", "row"),
        P(("enc", "col"), "row"),
        P(("enc", "col"), "row"),
        P("row", ("enc", "col")),
        P(None, ("enc", "col")),
        P("row", ("enc", "col")),
        P(),
        P(),
    )
    return jax.shard_map(
        shards, mesh=mesh, in_specs=placed, out_specs=P(None, ("enc", "col")), check_vma=False
    )
```

profile of v0, /device:TPU:0, one launch (start us, length us, event | category | flops | bytes accessed | tf_op | source)
XLA Modules:
  0.0 432.5 jit_solution(12022463329798389478)
XLA Ops:
  6.6 0.8 copy-done
  7.4 9.9 %fusion.25 = f32[48,7392]{1,0:T(8,128)S(1)} fusion(bf16[48,1024]{1,0:T(8,128)(2,1)S(1)} %copy-done, bf16[7392,1024]{1,0:T(8,128)(2,1)} %param.17), kind=kOutput, calls=%fused_computation.36 | convolution fusion | flops 726663168 | bytes 16656384 | tf_op jit(solution)/shard_map/dot_general | solution.py:12
  17.3 22.6 %fusion = f32[16,7392]{1,0:T(8,128)S(1)} fusion(f32[48,7392]{1,0:T(8,128)S(1)} %fusion.25), kind=kCustom, calls=%all-reduce-scatter | all-reduce-scatter fusion | flops 473089 | bytes 1892864
  40.0 1.3 collective-permute-start
  44.8 9.3 %fusion.1 = f32[8,7392]{1,0:T(8,128)S(1)} fusion(f32[12,7392]{1,0:T(8,128)S(1)} %constant_dynamic-slice_fusion), kind=kCustom, calls=%all-reduce-scatter.1 | all-reduce-scatter fusion | flops 118273 | bytes 591872
  54.1 2.4 collective-permute-start.1
  56.5 1.8 collective-permute-done.1
  58.9 6.2 %all-gather.2 = bf16[2,6,7392]{2,1,0:T(8,128)(2,1)S(1)} all-gather(bf16[1,6,7392]{2,1,0:T(8,128)(2,1)S(1)} %get-tuple-element.6), channel_id=1, replica_groups=mesh['enc'=4,'row'=4,'col'=2] {'col'}, dimensions={0}, use_global_device_ids=true | all-gather | bytes 266112 | tf_op jit(solution)/shard_map/all_gather | solution.py:43
  65.2 6.8 %all-gather = bf16[2,6,7392]{2,1,0:T(8,128)(2,1)S(1)} all-gather(bf16[1,6,7392]{2,1,0:T(8,128)(2,1)S(1)} %get-tuple-element.7), channel_id=1, replica_groups=mesh['enc'=4,'row'=4,'col'=2] {'col'}, dimensions={0}, use_global_device_ids=true | all-gather | bytes 266112 | tf_op jit(solution)/shard_map/all_gather | solution.py:42
  72.2 13.2 %all-gather.1 = bf16[4,12,7392]{2,1,0:T(8,128)(2,1)S(1)} all-gather(bf16[1,12,7392]{2,1,0:T(8,128)(2,1)S(1)} %reshape.47), channel_id=1, replica_groups=mesh['enc'=4,'row'=4,'col'=2] {'enc'}, dimensions={0}, use_global_device_ids=true | all-gather | bytes 887040 | tf_op jit(solution)/shard_map/all_gather | solution.py:46
  85.7 9.6 %all-gather.3 = bf16[4,12,7392]{2,1,0:T(8,128)(2,1)S(1)} all-gather(bf16[1,12,7392]{2,1,0:T(8,128)(2,1)S(1)} %reshape.51), channel_id=1, replica_groups=mesh['enc'=4,'row'=4,'col'=2] {'enc'}, dimensions={0}, use_global_device_ids=true | all-gather | bytes 887040 | tf_op jit(solution)/shard_map/all_gather | solution.py:47
  95.7 1.0 gather_fusion
  96.7 1.0 gather_fusion.1
  97.7 8.1 %fusion.5 = f32[48,1024]{1,0:T(8,128)S(1)} fusion(bf16[1024,7392]{0,1:T(8,128)(2,1)} %param.15, bf16[48,7392]{1,0:T(8,128)(2,1)S(1)} %gather_fusion, pred[48]{0:T(512)(128)(4,1)S(1)} %compare_and_fusion), kind=kOutput, calls=%fused_computation.7 | convolution fusion | flops 727017984 | bytes 16045104 | tf_op jit(solution)/shard_map/dot_general | solution.py:12
  105.8 8.1 %fusion.3 = f32[48,1024]{1,0:T(8,128)S(1)} fusion(f32[48,1024]{1,0:T(8,128)S(1)} %fusion.5, bf16[1024,7392]{0,1:T(8,128)(2,1)} %param.16, bf16[48,7392]{1,0:T(8,128)(2,1)S(1)} %gather_fusion.1, pred[48]{0:T(512)(128)(4,1)S(1)} %compare_and_fusion, pred[48]{0:T(512)(128)(4,1)S(1)} %fusion.22), kind=kOutput, calls=%fused_computation.5 | convolution fusion | flops 727116288 | bytes 16241760 | tf_op jit(solution)/shard_map/dot_general | solution.py:12
  114.0 15.4 %fusion.2 = f32[16,1024]{1,0:T(8,128)S(1)} fusion(f32[48,1024]{1,0:T(8,128)S(1)} %fusion.3), kind=kCustom, calls=%all-reduce-scatter.2 | all-reduce-scatter fusion | flops 65537 | bytes 262656
  129.4 2.0 collective-permute-start.2
  133.2 14.8 %convolution_bitcast_fusion = f32[12800,12]{1,0:T(8,128)} fusion(bf16[12800,1024]{1,0:T(8,128)(2,1)} %param.18, bf16[28,1024]{1,0:T(8,128)(2,1)S(1)} %concatenate.2, u32[]{:S(6)} %subtract.2), kind=kOutput, calls=%fused_computation.2 | convolution fusion | flops 314572800 | bytes 26861572
  148.1 63.3 %reduce-scatter.10.cloned.1.call-done = f32[1600,12]{1,0:T(8,128)} async-done(((f32[12800,12]{1,0:T(8,128)}), f32[1600,12]{1,0:T(8,128)}) %reduce-scatter.10.cloned.1.call-update) | async-done | bytes 76816
  211.4 1.4 copy.18
  213.5 17.0 %all-gather.4 = bf16[8,400,48]{1,2,0:T(8,128)(2,1)S(1)} all-gather(bf16[1,400,48]{1,2,0:T(8,128)(2,1)S(1)} %bitcast.33), channel_id=1, replica_groups=mesh['enc'=4,'row'=4,'col'=2] {'enc','col'}, dimensions={0}, use_global_device_ids=true | all-gather | bytes 345600 | tf_op jit(solution)/shard_map/all_gather | solution.py:71
  231.3 3.9 multiply_convert_fusion
  235.2 185.4 %all-reduce.8.cloned.1.call-done = bf16[3200,800]{0,1:T(8,128)(2,1)} async-done(((bf16[3200,800]{0,1:T(8,128)(2,1)}), bf16[3200,800]{0,1:T(8,128)(2,1)}) %all-reduce.8.cloned.1.call-update) | async-done | bytes 5120016 | tf_op jit(solution)/shard_map/psum | solution.py:74
  420.5 5.1 %copy.20 = bf16[3200,800]{0,1:T(8,128)(2,1)} copy(bf16[3200,800]{0,1:T(8,128)(2,1)} %all-reduce.8.cloned.1.call-done) | data formatting | bytes 10240000
  (51 shorter events, 6.2 us)
Async XLA Ops:
  6.5 0.9 copy-start
  6.5 34.8 %copy-start.8 = (u32[32]{0:T(128)S(1)}, u32[32]{0:T(128)}, u32[]{:S(2)}) copy-start(u32[32]{0:T(128)} %constant.41) | copy-start | bytes 388
  6.5 36.0 %copy-start.7 = (u32[32]{0:T(128)S(1)}, u32[32]{0:T(128)}, u32[]{:S(2)}) copy-start(u32[32]{0:T(128)} %constant.37) | copy-start | bytes 388
  6.5 36.6 %copy-start.9 = (s32[48]{0:T(128)S(1)}, s32[48]{0:T(128)}, u32[]{:S(2)}) copy-start(s32[48]{0:T(128)} %param.20) | copy-start | bytes 580
  6.5 36.6 %copy-start.5 = (s32[4]{0:T(128)S(1)}, s32[4]{0:T(128)}, u32[]{:S(2)}) copy-start(s32[4]{0:T(128)} %param.21) | copy-start | bytes 52
  6.5 52.1 %copy-start.4 = (bf16[12,7392]{1,0:T(8,128)(2,1)S(1)}, bf16[12,7392]{1,0:T(8,128)(2,1)}, u32[]{:S(2)}) copy-start(bf16[12,7392]{1,0:T(8,128)(2,1)} %param.14) | copy-start | bytes 532228
  6.6 52.1 %copy-start.3 = (bf16[12,7392]{1,0:T(8,128)(2,1)S(1)}, bf16[12,7392]{1,0:T(8,128)(2,1)}, u32[]{:S(2)}) copy-start(bf16[12,7392]{1,0:T(8,128)(2,1)} %param.13) | copy-start | bytes 532228
  6.6 204.9 %reduce-scatter.10.cloned.1.call-start = ((), (), s32[]{:S(2)}) async-start(), calls=%async_computation.2 | async-start | bytes 7372800
  40.0 4.0 collective-permute-start
  54.1 4.2 collective-permute-start.1
  105.8 25.7 %copy-start.6 = (u32[32]{0:T(128)S(1)}, u32[32]{0:T(128)}, u32[]{:S(2)}) copy-start(u32[32]{0:T(128)} %constant.45) | copy-start | bytes 388
  129.4 3.6 collective-permute-start.2
  133.2 98.1 %copy-start.2 = (bf16[48,800]{1,0:T(8,128)(2,1)S(1)}, bf16[48,800]{1,0:T(8,128)(2,1)}, u32[]{:S(2)}) copy-start(bf16[48,800]{1,0:T(8,128)(2,1)} %param.19) | copy-start | bytes 230404
  148.0 277.6 %copy-start.1 = (bf16[48,1024]{1,0:T(8,128)(2,1)S(1)}, bf16[48,1024]{1,0:T(8,128)(2,1)}, u32[]{:S(2)}) copy-start(bf16[48,1024]{1,0:T(8,128)(2,1)} %param.12) | copy-start | bytes 294916
  148.0 272.5 %all-reduce.8.cloned.1.call-start = ((), (), s32[]{:S(2)}) async-start(), calls=%async_computation.1 | async-start | bytes 10240000 | tf_op jit(solution)/shard_map/psum | solution.py:74
Sparse Core Ops, SparseCore 0:
  148.2 63.2 reduce-scatter.9
  235.3 185.2 all-reduce.7
where the time goes:
time: 433 us
  waiting for transfers between devices  251 us (58%)
  blocking collectives  100 us (23%)
  matrix products  44.8 us (10%)
  between operations  15.7 us (4%)
  local copies, waits for them, and re-layouts  15 us (3%)
  starting transfers between devices  5.85 us (1%)
    psum x1, waiting for transfers between devices, shards(): total = lax.psum(group_term.astype(jnp.bfloat16), 'row')  185 us
    unnamed x6, waiting for transfers between devices  65.5 us
    unnamed x3, blocking collectives  47.2 us
    dot_general x3, matrix products, contract_last(): lax.dot_general(left, right, (((1,), (1,)), ((), ())), preferred_element_...  26.1 us
    all_gather x1, blocking collectives, shards(): lax.all_gather(patch_grad, ('enc', 'col'), axis=1, tiled=True)  17 us
    unnamed x1, matrix products  14.8 us
    all_gather x1, blocking collectives, shards(): lax.all_gather(grad_gate, 'enc', axis=0, tiled=True)  13.2 us
    unnamed x37, local copies, waits for them, and re-layouts  11.9 us
  transfers between devices with their start and end apart: 5, of which 4 were waited for; matrix products, arithmetic and copies ran while one was open for 0% of the time, Pallas kernels for 0%

commit v1 on v0

--- a/solution.py
+++ b/solution.py
@@ -71,7 +71,9 @@
         contract_first(lax.all_gather(patch_grad, ("enc", "col"), axis=1, tiled=True), enc_hidden)
         * scale
     )
-    total = lax.psum(group_term.astype(jnp.bfloat16), "row")
+    own = group_term.astype(jnp.bfloat16)
+    parts = lax.all_gather(own, "row", axis=0, tiled=False)
+    total = parts.sum(axis=0)
     return total
 
 

time: 433 us -> 656 us (1.52)
  waiting for transfers between devices: 251 us -> 414 us
  other arithmetic: 0.23 us -> 30.5 us
  local copies, waits for them, and re-layouts: 15 us -> 43.7 us
    all_gather x0 -> x1, waiting for transfers between devices: none -> 349 us  [shards(): parts = lax.all_gather(own, 'row', axis=0, tiled=False)]
    psum x1 -> x0, waiting for transfers between devices: 185 us -> none  [shards(): total = lax.psum(group_term.astype(jnp.bfloat16), 'row')]
    all_gather x0 -> x1, local copies, waits for them, and re-layouts: none -> 33.8 us  [shards(): parts = lax.all_gather(own, 'row', axis=0, tiled=False)]
    reduce_sum x0 -> x1, other arithmetic: none -> 30.3 us  [shards(): total = parts.sum(axis=0)]
where the time goes in v1:
time: 656 us; the launch traced here: 655 us
  waiting for transfers between devices  414 us (63%)
  blocking collectives  100 us (15%)
  matrix products  44.8 us (7%)
  local copies, waits for them, and re-layouts  43.7 us (7%)
  other arithmetic  30.5 us (5%)
  between operations  15.7 us (2%)
    all_gather x1, waiting for transfers between devices, shards(): parts = lax.all_gather(own, 'row', axis=0, tiled=False)  349 us
    unnamed x6, waiting for transfers between devices  65.5 us
    unnamed x3, blocking collectives  47.2 us
    all_gather x1, local copies, waits for them, and re-layouts, shards(): parts = lax.all_gather(own, 'row', axis=0, tiled=False)  33.8 us
    reduce_sum x1, other arithmetic, shards(): total = parts.sum(axis=0)  30.3 us
    dot_general x3, matrix products, contract_last(): lax.dot_general(left, right, (((1,), (1,)), ((), ())), preferred_element_...  26.1 us
    all_gather x1, blocking collectives, shards(): lax.all_gather(patch_grad, ('enc', 'col'), axis=1, tiled=True)  17 us
    unnamed x1, matrix products  14.8 us
  transfers between devices with their start and end apart: 5, of which 4 were waited for; matrix products, arithmetic and copies ran while one was open for 0% of the time, Pallas kernels for 0%

profile of v1, /device:TPU:0, one launch (start us, length us, event | category | flops | bytes accessed | tf_op | source)
XLA Modules:
  0.0 655.0 jit_solution(10957209178124227281)
XLA Ops:
  7.4 9.9 %fusion.25 = f32[48,7392]{1,0:T(8,128)S(1)} fusion(bf16[48,1024]{1,0:T(8,128)(2,1)S(1)} %copy-done, bf16[7392,1024]{1,0:T(8,128)(2,1)} %param.17), kind=kOutput, calls=%fused_computation.36 | convolution fusion | flops 726663168 | bytes 16656384 | tf_op jit(solution)/shard_map/dot_general | solution.py:12
  17.3 22.6 %fusion = f32[16,7392]{1,0:T(8,128)S(1)} fusion(f32[48,7392]{1,0:T(8,128)S(1)} %fusion.25), kind=kCustom, calls=%all-reduce-scatter | all-reduce-scatter fusion | flops 473089 | bytes 1892864
  40.0 1.3 collective-permute-start
  44.8 9.3 %fusion.1 = f32[8,7392]{1,0:T(8,128)S(1)} fusion(f32[12,7392]{1,0:T(8,128)S(1)} %constant_dynamic-slice_fusion), kind=kCustom, calls=%all-reduce-scatter.1 | all-reduce-scatter fusion | flops 118273 | bytes 591872
  54.1 2.4 collective-permute-start.1
  56.5 1.8 collective-permute-done.1
  58.9 6.2 all-gather.3
  65.2 6.8 %all-gather.1 = bf16[2,6,7392]{2,1,0:T(8,128)(2,1)S(1)} all-gather(bf16[1,6,7392]{2,1,0:T(8,128)(2,1)S(1)} %get-tuple-element.7), channel_id=1, replica_groups=mesh['enc'=4,'row'=4,'col'=2] {'col'}, dimensions={0}, use_global_device_ids=true | all-gather | bytes 266112 | tf_op jit(solution)/shard_map/all_gather | solution.py:42
  72.2 13.2 %all-gather.2 = bf16[4,12,7392]{2,1,0:T(8,128)(2,1)S(1)} all-gather(bf16[1,12,7392]{2,1,0:T(8,128)(2,1)S(1)} %reshape.48), channel_id=1, replica_groups=mesh['enc'=4,'row'=4,'col'=2] {'enc'}, dimensions={0}, use_global_device_ids=true | all-gather | bytes 887040 | tf_op jit(solution)/shard_map/all_gather | solution.py:46
  85.7 9.6 %all-gather.4 = bf16[4,12,7392]{2,1,0:T(8,128)(2,1)S(1)} all-gather(bf16[1,12,7392]{2,1,0:T(8,128)(2,1)S(1)} %reshape.52), channel_id=1, replica_groups=mesh['enc'=4,'row'=4,'col'=2] {'enc'}, dimensions={0}, use_global_device_ids=true | all-gather | bytes 887040 | tf_op jit(solution)/shard_map/all_gather | solution.py:47
  95.7 1.0 gather_fusion
  96.7 1.0 gather_fusion.1
  97.7 8.1 %fusion.5 = f32[48,1024]{1,0:T(8,128)S(1)} fusion(bf16[1024,7392]{0,1:T(8,128)(2,1)} %param.15, bf16[48,7392]{1,0:T(8,128)(2,1)S(1)} %gather_fusion, pred[48]{0:T(512)(128)(4,1)S(1)} %compare_and_fusion), kind=kOutput, calls=%fused_computation.7 | convolution fusion | flops 727017984 | bytes 16045104 | tf_op jit(solution)/shard_map/dot_general | solution.py:12
  105.8 8.1 %fusion.3 = f32[48,1024]{1,0:T(8,128)S(1)} fusion(f32[48,1024]{1,0:T(8,128)S(1)} %fusion.5, bf16[1024,7392]{0,1:T(8,128)(2,1)} %param.16, bf16[48,7392]{1,0:T(8,128)(2,1)S(1)} %gather_fusion.1, pred[48]{0:T(512)(128)(4,1)S(1)} %compare_and_fusion, pred[48]{0:T(512)(128)(4,1)S(1)} %fusion.22), kind=kOutput, calls=%fused_computation.5 | convolution fusion | flops 727116288 | bytes 16241760 | tf_op jit(solution)/shard_map/dot_general | solution.py:12
  114.0 15.4 %fusion.2 = f32[16,1024]{1,0:T(8,128)S(1)} fusion(f32[48,1024]{1,0:T(8,128)S(1)} %fusion.3), kind=kCustom, calls=%all-reduce-scatter.2 | all-reduce-scatter fusion | flops 65537 | bytes 262656
  129.4 2.0 collective-permute-start.2
  133.2 14.8 %convolution_bitcast_fusion = f32[12800,12]{1,0:T(8,128)} fusion(bf16[12800,1024]{1,0:T(8,128)(2,1)} %param.18, bf16[28,1024]{1,0:T(8,128)(2,1)S(1)} %concatenate.2, u32[]{:S(6)} %subtract.2), kind=kOutput, calls=%fused_computation.2 | convolution fusion | flops 314572800 | bytes 26861572
  148.1 63.3 %reduce-scatter.10.cloned.1.call-done = f32[1600,12]{1,0:T(8,128)} async-done(((f32[12800,12]{1,0:T(8,128)}), f32[1600,12]{1,0:T(8,128)}) %reduce-scatter.10.cloned.1.call-update) | async-done | bytes 76816
  211.4 1.4 copy.18
  213.5 17.0 %all-gather.5 = bf16[8,400,48]{1,2,0:T(8,128)(2,1)S(1)} all-gather(bf16[1,400,48]{1,2,0:T(8,128)(2,1)S(1)} %bitcast.35), channel_id=1, replica_groups=mesh['enc'=4,'row'=4,'col'=2] {'enc','col'}, dimensions={0}, use_global_device_ids=true | all-gather | bytes 345600 | tf_op jit(solution)/shard_map/all_gather | solution.py:71
  231.3 3.9 multiply_convert_fusion
  235.2 349.0 %all-gather.8.cloned.1.call-done = bf16[12800,800]{0,1:T(8,128)(2,1)} async-done(((bf16[3200,800]{0,1:T(8,128)(2,1)}), bf16[12800,800]{0,1:T(8,128)(2,1)}) %all-gather.8.cloned.1.call-update) | async-done | bytes 20480016 | tf_op jit(solution)/shard_map/all_gather | solution.py:75
  584.1 33.8 %reshape.43 = bf16[4,3200,800]{1,0,2:T(4,128)(2,1)} reshape(bf16[12800,800]{0,1:T(8,128)(2,1)} %all-gather.8.cloned.1.call-done) | data formatting | bytes 40960000 | tf_op jit(solution)/shard_map/all_gather | solution.py:75
  617.9 30.3 %reduce_sum.12 = bf16[3200,800]{0,1:T(8,128)(2,1)} reduce(bf16[4,3200,800]{1,0,2:T(4,128)(2,1)} %reshape.43, bf16[]{:T(256)} %constant.37.clone.1), dimensions={0}, to_apply=%region_4.6 | reduce | flops 7680000 | bytes 25600002 | tf_op jit(solution)/shard_map/reduce_sum | solution.py:76
  (52 shorter events, 7.1 us)
Async XLA Ops:
  6.5 0.9 copy-start
  6.5 34.8 %copy-start.8 = (u32[32]{0:T(128)S(1)}, u32[32]{0:T(128)}, u32[]{:S(2)}) copy-start(u32[32]{0:T(128)} %constant.44) | copy-start | bytes 388
  6.5 36.0 %copy-start.7 = (u32[32]{0:T(128)S(1)}, u32[32]{0:T(128)}, u32[]{:S(2)}) copy-start(u32[32]{0:T(128)} %constant.40) | copy-start | bytes 388
  6.5 36.6 %copy-start.9 = (s32[48]{0:T(128)S(1)}, s32[48]{0:T(128)}, u32[]{:S(2)}) copy-start(s32[48]{0:T(128)} %param.20) | copy-start | bytes 580
  6.5 36.6 %copy-start.5 = (s32[4]{0:T(128)S(1)}, s32[4]{0:T(128)}, u32[]{:S(2)}) copy-start(s32[4]{0:T(128)} %param.21) | copy-start | bytes 52
  6.5 52.1 %copy-start.4 = (bf16[12,7392]{1,0:T(8,128)(2,1)S(1)}, bf16[12,7392]{1,0:T(8,128)(2,1)}, u32[]{:S(2)}) copy-start(bf16[12,7392]{1,0:T(8,128)(2,1)} %param.14) | copy-start | bytes 532228
  6.6 52.1 %copy-start.3 = (bf16[12,7392]{1,0:T(8,128)(2,1)S(1)}, bf16[12,7392]{1,0:T(8,128)(2,1)}, u32[]{:S(2)}) copy-start(bf16[12,7392]{1,0:T(8,128)(2,1)} %param.13) | copy-start | bytes 532228
  6.6 204.9 %reduce-scatter.10.cloned.1.call-start = ((), (), s32[]{:S(2)}) async-start(), calls=%async_computation.2 | async-start | bytes 7372800
  40.0 4.0 collective-permute-start
  54.1 4.2 collective-permute-start.1
  105.8 25.7 %copy-start.6 = (u32[32]{0:T(128)S(1)}, u32[32]{0:T(128)}, u32[]{:S(2)}) copy-start(u32[32]{0:T(128)} %constant.48) | copy-start | bytes 388
  129.4 3.6 collective-permute-start.2
  133.2 98.1 %copy-start.2 = (bf16[48,800]{1,0:T(8,128)(2,1)S(1)}, bf16[48,800]{1,0:T(8,128)(2,1)}, u32[]{:S(2)}) copy-start(bf16[48,800]{1,0:T(8,128)(2,1)} %param.19) | copy-start | bytes 230404
  148.0 436.1 %all-gather.8.cloned.1.call-start = ((), (), s32[]{:S(2)}) async-start(), calls=%async_computation.1 | async-start | bytes 25600000 | tf_op jit(solution)/shard_map/all_gather | solution.py:75
  584.1 64.1 %copy-start.1 = (bf16[48,1024]{1,0:T(8,128)(2,1)S(1)}, bf16[48,1024]{1,0:T(8,128)(2,1)}, u32[]{:S(2)}) copy-start(bf16[48,1024]{1,0:T(8,128)(2,1)} %param.12) | copy-start | bytes 294916
Sparse Core Ops, SparseCore 0:
  148.2 63.2 reduce-scatter.9
  235.3 348.7 all-gather.7
